TPU v7x, 256 devices: a whole 4x4x8 slice. The times are simulated.
256 devices in a mesh: dp: 64 (over z, y, x_hi), mp: 4 (over x_lo, core).
Axes of the slice: x: 4 (x_hi: 2, x_lo: 2; x = x_hi * 2 + x_lo), y: 4, z: 8, core: 2. Of those that a mesh axis runs over, the one named last changes fastest.
Arguments:
- streams: bfloat16 [16384, 4, 8192], P('dp', None, 'mp'), may hold values from -200 to 200
- branch_out: bfloat16 [16384, 8192], P('dp', 'mp'), may hold values from -6 to 6
- merge_weight: float32 [20, 4, 8192], P(None, None, ('mp', 'dp')), may hold values from -0.03125 to 0.03125
- next_weight: float32 [24, 4, 8192], P(None, None, ('mp', 'dp')), may hold values from -0.03125 to 0.03125
- blend_bias: float32 [44], replicated, may hold values from -3 to 3
- blend_scale: float32 [5], replicated, may hold values from 0.5 to 3
- norm_gain: float32 [8192], P('mp'), may hold values from 0.5 to 1.5
Outputs:
- streams_out: bfloat16 [16384, 4, 8192], P('dp', None, 'mp')
- branch_in: bfloat16 [16384, 8192], P('dp', 'mp')
- next_mix: float32 [16384, 20], P('dp')
All inputs are finite; a program needn't handle non-finite values.
Results may differ from a plain program's by a relative error of at most 0.001.
Values sent between devices are 32-bit elements; how exact they have to be, the bound alone decides.
A program may use at most 64 MiB of HBM per device.

v0:
```python
import jax
import jax.numpy as jnp
from jax import lax
from jax.sharding import PartitionSpec as P

D = 8192
STREAMS = 4
BALANCE_ROUNDS = 6


epsilon = 1e-06


def copy_for_each(x, axis):
    peers = lax.axis_size(axis)
    return lax.all_to_all(jnp.broadcast_to(x[None], (peers, *x.shape)), axis, 0, 0, tiled=True)


def of_everyone(x, axis):
    everything = copy_for_each(x, axis)
    return jnp.sum(everything, axis=0)


def turned_gather(arrays, axis, dims):
    turned = [jnp.moveaxis(a, dim, 0) for a, dim in zip(arrays, dims)]
    both = jnp.concatenate([t.reshape(len(t), -1) for t in turned], axis=1)
    filled, at, gathered = (lax.all_gather(both, axis, axis=0, tiled=True), 0, [])
    for t, dim in zip(turned, dims):
        section = filled[:, at : at + t[0].size].reshape(-1, *t.shape[1:])
        gathered.append(jnp.moveaxis(section, 0, dim))
        at += t[0].size
    return tuple(gathered)


def balance_normalize(balanced_matrix):
    for balance_round in range(BALANCE_ROUNDS):
        balanced_matrix = balanced_matrix / jnp.sum(balanced_matrix, axis=2, keepdims=True)
        balanced_matrix = balanced_matrix / jnp.sum(balanced_matrix, axis=1, keepdims=True)
    return balanced_matrix


def settle(columns, finish):
    summed = of_everyone(columns, "mp")
    result = finish(summed)
    return result


def first_coef(raw_sums, squares, blend_bias, blend_scale):
    rms_root = jnp.sqrt(squares / (STREAMS * D) + epsilon)
    score_logits = raw_sums / rms_root[:, None]
    post_mix = 2.0 * jax.nn.sigmoid(blend_scale[0] * score_logits[:, :4] + blend_bias[:4])
    residual_blend = balance_normalize(
        jnp.exp(
            blend_scale[1] * score_logits[:, 4:20].reshape(-1, 4, 4)
            + blend_bias[4:20].reshape(4, 4)
        )
    )
    return (post_mix, residual_blend)


def second_coef(raw_sums, squares, blend_bias, blend_scale):
    rms_root = jnp.sqrt(squares / (STREAMS * D) + epsilon)
    score_logits = raw_sums / rms_root[:, None]
    pre_next = jax.nn.sigmoid(blend_scale[2] * score_logits[:, :4] + blend_bias[20:24])
    post_next = 2.0 * jax.nn.sigmoid(blend_scale[3] * score_logits[:, 4:8] + blend_bias[24:28])
    residual_following = balance_normalize(
        jnp.exp(
            blend_scale[4] * score_logits[:, 8:24].reshape(-1, 4, 4)
            + blend_bias[28:44].reshape(4, 4)
        )
    )
    return (pre_next, post_next, residual_following)


def mix_streams(residual_blend, post_mix, streams, branch_out):
    branch_wide = branch_out.astype(jnp.float32)
    outputs = []
    for target in range(STREAMS):
        total = post_mix[:, target, None] * branch_wide
        for source in range(STREAMS):
            total = total + residual_blend[:, target, source, None] * streams[:, source, :].astype(
                jnp.float32
            )
        outputs.append(total)
    return jnp.stack(outputs, axis=1)


def unite(pre_next, mixed):
    total = pre_next[:, 0, None] * mixed[:, 0, :]
    for source in range(1, STREAMS):
        total = total + pre_next[:, source, None] * mixed[:, source, :]
    return total


def local(streams, branch_out, merge_weight, next_weight, blend_bias, blend_scale, norm_gain):
    merge_rows, next_rows = turned_gather((merge_weight, next_weight), "dp", (2, 2))
    highest = lax.Precision.HIGHEST
    raw_part = jnp.einsum(
        "tic,kic->tk", streams, merge_rows, precision=highest, preferred_element_type=jnp.float32
    )
    gram_part = jnp.einsum("tic,tjc->tij", streams, streams, preferred_element_type=jnp.float32)
    columns = jnp.concatenate([raw_part, jnp.trace(gram_part, axis1=1, axis2=2)[:, None]], axis=1)

    def finish_first(summed):
        post_mix, residual_blend = first_coef(
            summed[:, :20], summed[:, 20], blend_bias, blend_scale
        )
        return jnp.concatenate([post_mix, residual_blend.reshape(-1, 16)], axis=1)

    merge_coef = settle(columns, finish_first)
    post_mix = merge_coef[:, :4]
    residual_blend = merge_coef[:, 4:20].reshape(-1, 4, 4)
    mixed = mix_streams(residual_blend, post_mix, streams, branch_out)
    streams_out = mixed.astype(jnp.bfloat16)
    raw_next = jnp.einsum("tic,kic->tk", mixed, next_rows, precision=highest)
    extra_cols = jnp.sum(mixed * mixed, axis=(1, 2))[:, None]
    columns_next = jnp.concatenate([raw_next, extra_cols], axis=1)

    def finish_second(summed):
        squares = summed[:, 24]
        pre_next, post_next, residual_following = second_coef(
            summed[:, :24], squares, blend_bias, blend_scale
        )
        pieces = [pre_next, post_next, residual_following.reshape(-1, 16)]
        return jnp.concatenate(pieces, axis=1)

    next_coef = settle(columns_next, finish_second)
    pre_next = next_coef[:, :4]
    next_mix = next_coef[:, 4:24]
    united = unite(pre_next, mixed)
    united_sq = of_everyone(jnp.sum(united * united, axis=1), "mp")
    branch_in = (united / jnp.sqrt(united_sq / D + epsilon)[:, None] * norm_gain).astype(
        jnp.bfloat16
    )
    return (streams_out, branch_in, next_mix)


def solution(mesh):
    placed = (
        P("dp", None, "mp"),
        P("dp", "mp"),
        P(None, None, ("mp", "dp")),
        P(None, None, ("mp", "dp")),
        P(),
        P(),
        P("mp"),
    )
    return jax.shard_map(
        local,
        mesh=mesh,
        in_specs=placed,
        out_specs=(P("dp", None, "mp"), P("dp", "mp"), P("dp", None)),
        check_vma=False,
    )
```

profile of v0, /device:TPU:1, one launch (start us, length us, event | category | flops | bytes accessed | tf_op | source)
XLA Modules:
  0.0 209.4 jit_solution(10708887090275913820)
XLA Ops:
  7.2 0.0 all-gather.2.cloned.1.call-start
  7.2 0.8 copy.64
  8.1 0.9 copy.65
  8.9 0.7 pad_maximum_fusion.4
  9.6 0.0 all-gather.2.cloned.1.call-update
  9.7 0.8 fusion.84
  10.5 0.1 add.134
  10.5 0.1 add.166
  10.6 6.7 %copy.68 = bf16[256,4,2048]{2,0,1:T(8,128)(2,1)} copy(bf16[256,4,2048]{2,1,0:T(4,128)(2,1)} %param.7) | data formatting | bytes 8388608 | tf_op args[0]
  17.3 0.0 copy-done.7
  17.3 0.1 fusion.83
  17.4 0.0 copy-done.4
  17.4 5.8 %fusion.28 = f32[256]{0:T(256)S(1)} fusion(bf16[256,4,2048]{2,1,0:T(4,128)(2,1)S(1)} %copy-done.4, pred[4,4]{1,0:T(4,128)(4,1)S(1)} %iota_compare_fusion), kind=kOutput, calls=%fused_computation.54 | convolution fusion | flops 16785152 | bytes 4195344 | tf_op jit(solution)/shard_map/tic,tjc->tij/dot_general | solution.py:101
  23.1 107.6 %all-gather.2.cloned.1.call-done = f32[2048,176]{1,0:T(8,128)} async-done(((f32[32,176]{1,0:T(8,128)}), f32[2048,176]{1,0:T(8,128)}) %all-gather.2.cloned.1.call-update) | async-done | bytes 1441808 | tf_op jit(solution)/shard_map/all_gather | solution.py:27
  130.7 1.2 slice-done
  132.0 0.3 copy.66
  132.3 0.2 reshape.126
  132.5 0.0 copy-start.8
  132.5 9.7 %convolution_bitcast_fusion = f32[256,20]{0,1:T(8,128)S(1)} fusion(f32[2048,20,4]{0,2,1:T(4,128)S(1)} %reshape.126, bf16[256,4,2048]{2,1,0:T(4,128)(2,1)} %param.7), kind=kOutput, calls=%fused_computation.56 | convolution fusion | flops 503316480 | bytes 4870144 | tf_op jit(solution)/shard_map/tic,kic->tk/dot_general | solution.py:98
  142.2 0.6 broadcast_in_dim.22
  142.8 7.7 %all-to-all-start = ((f32[4,256,21]{1,2,0:T(8,128)}), f32[4,256,21]{1,2,0:T(8,128)S(1)}, u32[]{:S(2)}, u32[]{:S(2)}) async-start(f32[4,256,21]{1,2,0:T(8,128)} %broadcast_in_dim.22), calls=%async_computation | async-start | bytes 196608 | tf_op jit(solution)/shard_map/all_to_all | solution.py:16
  150.5 0.0 copy-done.8
  150.5 0.6 fusion.82
  151.2 1.9 slice.249
  153.1 0.3 copy.73
  153.4 0.0 copy-start.5
  153.4 1.1 reshape.127
  154.5 0.0 all-to-all-done
  154.6 0.6 slice_multiply_fusion.1
  155.2 0.8 fusion.60
  155.9 0.1 fusion.78
  156.3 0.0 copy-done.5
  156.3 0.0 copy-start
  156.4 4.0 %fusion.13 = (f32[256,2048]{1,0:T(8,128)S(1)}, f32[256,2048]{1,0:T(8,128)S(1)}) fusion(bf16[256,2048]{1,0:T(8,128)(2,1)S(1)} %copy-done.5, f32[256]{0:T(256)S(1)} %bitcast.153, f32[256]{0:T(256)S(1)} %bitcast.154, f32[256]{0:T(256)S(1)} %bitcast.155, f32[256]{0:T(256)S(1)} %bitcast.148, f32[256]{0:T(256)S(1)} %bitcast.158, bf16[256,4,2048]{2,0,1:T(8,128)(2,1)} %copy.68, ...), kind=kLoop, calls=%fused_computation.35 | loop fusion | flops 12058624 | bytes 9447424 | tf_op jit(solution)/shard_map/add | solution.py:81
  160.3 0.0 copy-start.1
  160.4 2.3 %fusion.21 = (f32[256,2048]{1,0:T(8,128)S(1)}, f32[256,2048]{1,0:T(8,128)S(1)}) fusion(bf16[256,2048]{1,0:T(8,128)(2,1)S(1)} %copy-done.5, f32[256]{0:T(256)S(1)} %bitcast.144, f32[256]{0:T(256)S(1)} %bitcast.145, f32[256]{0:T(256)S(1)} %bitcast.146, f32[256]{0:T(256)S(1)} %bitcast.147, f32[256]{0:T(256)S(1)} %bitcast.157, ...), kind=kLoop, calls=%fused_computation.43 | loop fusion | flops 12058624 | bytes 9447424 | tf_op jit(solution)/shard_map/add | solution.py:81
  162.7 0.0 copy-start.6
  162.7 0.9 multiply_reduce_fusion
  163.5 0.4 copy-done.2
  163.9 0.7 copy-done.3
  164.6 0.0 copy-done.6
  164.6 6.6 %fusion.29 = f32[256,24]{0,1:T(8,128)S(1)} fusion(f32[256,1,2048]{2,0,1:T(8,128)S(1)} %bitcast.128, f32[256,1,2048]{2,0,1:T(8,128)S(1)} %bitcast.125, f32[256,1,2048]{2,0,1:T(8,128)S(1)} %bitcast.122, f32[256,1,2048]{2,0,1:T(8,128)S(1)} %bitcast.119, f32[2048,24,4]{0,2,1:T(4,128)S(1)} %copy-done.6), kind=kOutput, calls=%fused_computation.55 | convolution fusion | flops 610271232 | bytes 9199616 | tf_op jit(solution)/shard_map/tic,kic->tk/dot_general | solution.py:115
  171.3 0.7 broadcast_in_dim.24
  171.9 3.6 %all-to-all-start.1 = ((f32[4,256,25]{1,2,0:T(8,128)}), f32[4,256,25]{1,2,0:T(8,128)S(1)}, u32[]{:S(2)}, u32[]{:S(2)}) async-start(f32[4,256,25]{1,2,0:T(8,128)} %broadcast_in_dim.24), calls=%async_computation.1 | async-start | bytes 262144 | tf_op jit(solution)/shard_map/all_to_all | solution.py:16
  175.5 3.2 %fusion.27 = bf16[256,4,2048]{2,0,1:T(8,128)(2,1)S(1)} fusion(f32[256,1,2048]{2,0,1:T(8,128)} %bitcast.129, f32[256,1,2048]{2,0,1:T(8,128)} %bitcast.126, f32[256,1,2048]{2,0,1:T(8,128)} %bitcast.123, f32[256,1,2048]{2,0,1:T(8,128)S(1)} %bitcast.120), kind=kLoop, calls=%fused_computation.52 | loop fusion | flops 6291456 | bytes 12582912 | tf_op jit(solution)/shard_map/convert_element_type | solution.py:114
  178.8 5.3 %copy.76 = bf16[256,4,2048]{2,1,0:T(4,128)(2,1)} copy(bf16[256,4,2048]{2,0,1:T(8,128)(2,1)S(1)} %fusion.27) | data formatting | bytes 8388608
  184.0 0.0 all-to-all-done.1
  184.1 1.3 fusion.49
  185.4 0.6 slice_multiply_fusion
  186.1 0.1 fusion.76
  186.2 0.1 divide_reduce_fusion
  186.2 0.1 divide_reduce_fusion.6
  186.4 0.1 divide_reduce_fusion.5
  186.5 0.1 divide_reduce_fusion.4
  186.6 0.1 divide_reduce_fusion.3
  186.7 0.1 divide_reduce_fusion.2
  186.8 0.7 exponential_divide_fusion
  187.6 0.0 copy-start.9
  187.6 4.9 %multiply_reduce_fusion.1 = (f32[256]{0:T(256)S(1)}, f32[256,2048]{1,0:T(8,128)}) fusion(f32[256,2048]{1,0:T(8,128)} %copy-done.3, f32[256]{0:T(256)S(1)} %bitcast.161, f32[256,2048]{1,0:T(8,128)} %copy-done.2, f32[256]{0:T(256)S(1)} %bitcast.162, f32[256,2048]{1,0:T(8,128)} %copy-done.1, f32[256]{0:T(256)S(1)} %bitcast.163, ...), kind=kLoop, calls=%fused_computation.49 | loop fusion | flops 4718336 | bytes 10490880 | tf_op jit(solution)/shard_map/reduce_sum | solution.py:131
  192.5 0.6 broadcast_in_dim.25
  193.1 3.5 %all-to-all-start.2 = ((f32[4,1,256]{2,1,0:T(1,128)}), f32[4,1,256]{2,1,0:T(1,128)S(1)}, u32[]{:S(2)}, u32[]{:S(2)}) async-start(f32[4,1,256]{2,1,0:T(1,128)} %broadcast_in_dim.25), calls=%async_computation.2 | async-start | bytes 8192 | tf_op jit(solution)/shard_map/all_to_all | solution.py:16
  196.5 0.6 pad_maximum_fusion.7
  197.2 2.5 %all-to-all-done.2 = f32[4,1,256]{2,1,0:T(1,128)S(1)} async-done(((f32[4,1,256]{2,1,0:T(1,128)}), f32[4,1,256]{2,1,0:T(1,128)S(1)}, u32[]{:S(2)}, u32[]{:S(2)}) %all-to-all-start.2) | async-done | bytes 4128 | tf_op jit(solution)/shard_map/all_to_all | solution.py:16
  199.7 2.9 %multiply_convert_fusion = bf16[256,2048]{1,0:T(8,128)(2,1)} fusion(f32[256,2048]{1,0:T(8,128)} %get-tuple-element.22, f32[2048]{0:T(1024)S(1)} %copy-done.9, f32[256]{0:T(256)S(1)} %add_sqrt_fusion), kind=kLoop, calls=%fused_computation.48 | loop fusion | flops 1572864 | bytes 3154944 | tf_op jit(solution)/shard_map/convert_element_type | solution.py:132
  (35 shorter events, 0.4 us)
Async XLA Ops:
  7.2 123.6 %all-gather.2.cloned.1.call-start = ((), (), s32[]{:S(2)}) async-start(), calls=%async_computation.3 | async-start | bytes 2129920 | tf_op jit(solution)/shard_map/all_gather | solution.py:27
  10.6 6.7 %copy-start.7 = (f32[44]{0:T(128)S(1)}, f32[44]{0:T(128)}, u32[]{:S(2)}) copy-start(f32[44]{0:T(128)} %param.11) | copy-start | bytes 532
  10.6 6.7 %copy-start.4 = (bf16[256,4,2048]{2,1,0:T(4,128)(2,1)S(1)}, bf16[256,4,2048]{2,1,0:T(4,128)(2,1)}, u32[]{:S(2)}) copy-start(bf16[256,4,2048]{2,1,0:T(4,128)(2,1)} %param.7) | copy-start | bytes 12582916
  130.7 1.2 slice-start
  132.5 18.1 %copy-start.8 = (f32[5]{0:T(128)S(1)}, f32[5]{0:T(128)}, u32[]{:S(2)}) copy-start(f32[5]{0:T(128)} %param.12) | copy-start | bytes 64
  142.8 11.7 %all-to-all-start = ((f32[4,256,21]{1,2,0:T(8,128)}), f32[4,256,21]{1,2,0:T(8,128)S(1)}, u32[]{:S(2)}, u32[]{:S(2)}) async-start(f32[4,256,21]{1,2,0:T(8,128)} %broadcast_in_dim.22), calls=%async_computation | async-start | bytes 196608 | tf_op jit(solution)/shard_map/all_to_all | solution.py:16
  153.4 2.9 %copy-start.5 = (bf16[256,2048]{1,0:T(8,128)(2,1)S(1)}, bf16[256,2048]{1,0:T(8,128)(2,1)}, u32[]{:S(2)}) copy-start(bf16[256,2048]{1,0:T(8,128)(2,1)} %param.8) | copy-start | bytes 3145732
  156.3 4.0 %copy-start = (bf16[256,4,2048]{2,0,1:T(8,128)(2,1)S(1)}, bf16[256,4,2048]{2,0,1:T(8,128)(2,1)}, u32[]{:S(2)}) copy-start(bf16[256,4,2048]{2,0,1:T(8,128)(2,1)} %copy.68) | copy-start | bytes 12582916
  160.3 3.2 %copy-start.1 = (f32[256,2048]{1,0:T(8,128)}, f32[256,2048]{1,0:T(8,128)S(1)}, u32[]{:S(2)}) copy-start(f32[256,2048]{1,0:T(8,128)S(1)} %get-tuple-element.26) | copy-start | bytes 6291460
  162.6 1.3 copy-start.2
  162.6 2.0 copy-start.3
  162.7 2.0 copy-start.6
  171.9 12.1 %all-to-all-start.1 = ((f32[4,256,25]{1,2,0:T(8,128)}), f32[4,256,25]{1,2,0:T(8,128)S(1)}, u32[]{:S(2)}, u32[]{:S(2)}) async-start(f32[4,256,25]{1,2,0:T(8,128)} %broadcast_in_dim.24), calls=%async_computation.1 | async-start | bytes 262144 | tf_op jit(solution)/shard_map/all_to_all | solution.py:16
  187.6 12.1 %copy-start.9 = (f32[2048]{0:T(1024)S(1)}, f32[2048]{0:T(1024)}, u32[]{:S(2)}) copy-start(f32[2048]{0:T(1024)} %param.13) | copy-start | bytes 24580
  193.1 6.6 %all-to-all-start.2 = ((f32[4,1,256]{2,1,0:T(1,128)}), f32[4,1,256]{2,1,0:T(1,128)S(1)}, u32[]{:S(2)}, u32[]{:S(2)}) async-start(f32[4,1,256]{2,1,0:T(1,128)} %broadcast_in_dim.25), calls=%async_computation.2 | async-start | bytes 8192 | tf_op jit(solution)/shard_map/all_to_all | solution.py:16
Sparse Core Ops, SparseCore 0:
  12.1 118.5 all-gather.1
where the time goes:
time: 210 us; the launch traced here: 209 us
  waiting for transfers between devices  110 us (52%)
  other arithmetic  24.6 us (12%)
  local copies, waits for them, and re-layouts  23.5 us (11%)
  matrix products  22.1 us (11%)
  starting transfers between devices  14.8 us (7%)
  between operations  14.4 us (7%)
    all_gather x1, waiting for transfers between devices, turned_gather(): lax.all_gather(both, axis, axis=0, tiled=True)  108 us
    all_to_all x3, starting transfers between devices, copy_for_each(): lax.all_to_all(jnp.broadcast_to(x[None], (peers, *x.shape)), axis, 0, 0,...  14.8 us
    unnamed x24, local copies, waits for them, and re-layouts  13 us
    dot_general x1, matrix products, local(): jnp.einsum('tic,kic->tk', streams, merge_rows, precision=highest, preferr...  9.68 us
    dot_general x1, matrix products, local(): raw_next = jnp.einsum('tic,kic->tk', mixed, next_rows, precision=highest)  6.63 us
    add x2, other arithmetic, mix_streams(): total + residual_blend[:, target, source, None] * streams[:, source, :].a...  6.25 us
    dot_general x1, matrix products, local(): jnp.einsum('tic,tjc->tij', streams, streams, preferred_element_type=jnp.f...  5.77 us
    reduce_sum x1, other arithmetic, local(): united_sq = of_everyone(jnp.sum(united * united, axis=1), 'mp')  4.89 us
  transfers between devices with their start and end apart: 4, of which 2 were waited for; matrix products, arithmetic and copies ran while one was open for 13% of the time, Pallas kernels for 0%

commit v1 on v0

v1 whole, which is shorter than its diff:
```python
import jax
import jax.numpy as jnp
from jax import lax
from jax.experimental import pallas as pl
from jax.experimental.pallas import tpu as pltpu
from jax.sharding import PartitionSpec as P

D = 8192
STREAMS = 4
BALANCE_ROUNDS = 6
EPS = 1e-06

NZ = 8
NP = 8
NDP = NZ * NP
NMP = 4
TOK = 256
FEAT = 2048
TB = 32
NB = TOK // TB
SR = TB * STREAMS
XR = SR + TB
K = 24
MESH = pl.DeviceIdType.MESH
F32 = jnp.float32
BF16 = jnp.bfloat16

NT = (((1,), (1,)), ((), ()))
NN = (((1,), (0,)), ((), ()))


def dot(a, b, dims):
    return lax.dot_general(a, b, dims, preferred_element_type=F32)


def iota(shape, dim):
    return lax.broadcasted_iota(jnp.int32, shape, dim)


def split2(x):
    hi = x.astype(BF16).astype(F32)
    return [hi, x - hi]


def split3(x):
    hi = x.astype(BF16).astype(F32)
    rest = x - hi
    mid = rest.astype(BF16).astype(F32)
    return [hi, mid, rest - mid]


def pieces(parts):
    return jnp.concatenate(parts, axis=0).astype(BF16)


def token_of(u):
    return jnp.where(u < SR, u >> 2, jnp.where(u < XR, u - SR, -1))


def part_of(u):
    return jnp.where(u < SR, u & 3, STREAMS)


def block_rows(sb, bb, b):
    s3 = sb.reshape(16, TOK * STREAMS, 128)
    rows = pl.ds(pl.multiple_of(b * SR, SR), SR)
    brows = pl.ds(pl.multiple_of(b * TB, TB), TB)
    return s3, rows, brows


def balance(m):
    first = True
    for _ in range(BALANCE_ROUNDS):
        for j in range(4):
            total = (m[j][0] + m[j][1]) + (m[j][2] + m[j][3])
            if first:
                m[j] = [v / total for v in m[j]]
            else:
                inv = 1.0 / total
                m[j] = [v * inv for v in m[j]]
        first = False
        invs = [1.0 / ((m[0][i] + m[1][i]) + (m[2][i] + m[3][i])) for i in range(4)]
        m = [[m[j][i] * invs[i] for i in range(4)] for j in range(4)]
    return m


def gram_row(gt, a, b):
    a, b = min(a, b), max(a, b)
    row = b * (b + 1) // 2 + a
    return gt[row : row + 1, :]


def spread(rows5, rep5):
    d = dot(pieces(split2(rows5)), rep5[...], NN)
    part = part_of(iota((8, NB * 256), 1) & 255)
    out = []
    for base in (0, 40):
        v = d[base + 32 : base + 40]
        for a in range(4):
            v = jnp.where(part == a, d[base + 8 * a : base + 8 * a + 8], v)
        out.append(v)
    return out


def gather_kernel(
    s_hbm, b_hbm, w0_hbm, w1_hbm, bias, scale,
    sb, bb, ob, tot1, gt, cf, rep5,
    g, pacc, pbacc, rep4, w0v, w1v, gr, aexp, ex, exg, tot0,
    in_sem, ps, pr, rs, rr, es, er,
):
    dp = lax.axis_index("dp")
    mp = lax.axis_index("mp")
    z = dp // NP
    p = dp % NP
    up = lax.rem(z + 1, NZ)
    down = lax.rem(z + NZ - 1, NZ)

    def dev(d, m):
        return {"dp": d, "mp": m}

    wcopies = [
        pltpu.make_async_copy(w0_hbm, w0v, in_sem.at[0]),
        pltpu.make_async_copy(w1_hbm, w1v, in_sem.at[1]),
    ]
    for c in wcopies:
        c.start()
    icopies = [pltpu.make_async_copy(b_hbm, bb, in_sem.at[2])]
    for q in range(16):
        icopies.append(
            pltpu.make_async_copy(
                s_hbm.at[:, :, pl.ds(q * 128, 128)], sb.at[q], in_sem.at[3 + q]
            )
        )

    barrier = pltpu.get_barrier_semaphore()
    for o in range(1, NP):
        pl.semaphore_signal(
            barrier, inc=1, device_id=dev(z * NP + lax.rem(p + o, NP), mp), device_id_type=MESH
        )
    for zz in (up, down):
        pl.semaphore_signal(barrier, inc=1, device_id=dev(zz * NP + p, mp), device_id_type=MESH)
    for o in range(1, NMP):
        pl.semaphore_signal(
            barrier, inc=1, device_id=dev(dp, lax.rem(mp + o, NMP)), device_id_type=MESH
        )
    for c in icopies:
        c.start()

    for c in wcopies:
        c.wait()
    for i in range(STREAMS):
        g[0, dp, 0:20, 32 * i : 32 * i + 32] = w0v[:, i, :]
        g[1, dp, :, 32 * i : 32 * i + 32] = w1v[:, i, :]
    g[0, dp, 20:24, :] = jnp.zeros((4, 128), F32)
    pl.semaphore_wait(barrier, (NP - 1) + 2 + (NMP - 1))

    def plane(w, o, target, src):
        return pltpu.make_async_remote_copy(
            src_ref=g.at[w, src], dst_ref=g.at[w, src],
            send_sem=ps.at[w, o - 1], recv_sem=pr.at[w, o - 1],
            device_id=dev(z * NP + target, mp), device_id_type=MESH,
        )

    for w in range(2):
        for o in range(1, NP):
            plane(w, o, lax.rem(p + o, NP), dp).start()

    def hop(w, k, right, slab):
        idx = 0 if right else 1
        first = slab * NP
        ref = g.at[w, pl.ds(first, NP)]
        return pltpu.make_async_remote_copy(
            src_ref=ref, dst_ref=ref,
            send_sem=rs.at[idx, w, k - 1], recv_sem=rr.at[idx, w, k - 1],
            device_id=dev((up if right else down) * NP + p, mp), device_id_type=MESH,
        )

    def half_hop(w, right, slab):
        idx = 0 if right else 1
        first = slab * NP + (0 if right else NP // 2)
        ref = g.at[w, pl.ds(first, NP // 2)]
        return pltpu.make_async_remote_copy(
            src_ref=ref, dst_ref=ref,
            send_sem=rs.at[idx, w, 3], recv_sem=rr.at[idx, w, 3],
            device_id=dev((up if right else down) * NP + p, mp), device_id_type=MESH,
        )

    def exchange(ref, e, o, to, slot):
        return pltpu.make_async_remote_copy(
            src_ref=ref.at[slot], dst_ref=ref.at[slot],
            send_sem=es.at[e, o - 1], recv_sem=er.at[e, o - 1],
            device_id=dev(dp, to), device_id_type=MESH,
        )

    def exchange_start(ref, e):
        for o in range(1, NMP):
            exchange(ref, e, o, lax.rem(mp + o, NMP), mp).start()

    def exchange_wait(ref, e):
        for o in range(1, NMP):
            exchange(ref, e, o, lax.rem(mp + o, NMP), lax.rem(mp + NMP - o, NMP)).wait_recv()

    def plane_wait(w):
        for o in range(1, NP):
            plane(w, o, lax.rem(p + o, NP), z * NP + lax.rem(p + NP - o, NP)).wait_recv()

    tok = iota((TOK, TOK * STREAMS), 0)
    rep4[...] = jnp.where(tok == (iota((TOK, TOK * STREAMS), 1) >> 2), 1.0, 0.0).astype(BF16)
    for b in range(NB):
        u = iota((TOK, 256), 1)
        rep5[:, 256 * b : 256 * b + 256] = jnp.where(
            (iota((TOK, 256), 0) == b * TB + token_of(u)) & (u < XR), 1.0, 0.0
        ).astype(BF16)
    pacc[...] = jnp.zeros_like(pacc)
    pbacc[...] = jnp.zeros_like(pbacc)
    gr[...] = jnp.zeros_like(gr)
    for c in icopies:
        c.wait()

    plane_wait(0)
    hop(0, 1, True, z).start()
    hop(0, 1, False, z).start()
    plane_wait(1)
    hop(1, 1, True, z).start()
    hop(1, 1, False, z).start()

    def gram_block(b, carry):
        s3, rows, brows = block_rows(sb, bb, b)
        x = jnp.concatenate(
            [jnp.concatenate([s3[q, rows, :] for q in range(16)], axis=1), bb[brows, :]], axis=0
        )
        m = dot(x, x, NT)
        same = token_of(iota((XR, XR), 0)) == token_of(iota((XR, XR), 1))
        m = jnp.where(same, m, 0.0)
        top = jnp.sum(m[:SR].reshape(SR // 8, 8, XR), axis=0)
        low = jnp.sum(m[SR:], axis=0, keepdims=True)
        at = pl.multiple_of(b * 256, 256)
        gr[0:4, pl.ds(at, XR)] = top[0:4] + top[4:8]
        gr[4:5, pl.ds(at, XR)] = low
        return carry

    lax.fori_loop(0, NB, gram_block, 0)
    lanes5 = iota((8, NB * 256), 1) & 255
    part5 = part_of(lanes5)
    grv = gr[...]
    masked = [jnp.where(part5 == a, grv, 0.0) for a in range(5)]
    sums = dot(pieces(split3(jnp.concatenate(masked, axis=0))), rep5[...], NT)
    sums = sums[0:40] + sums[40:80] + sums[80:120]
    for b in range(5):
        row = b * (b + 1) // 2
        exg[mp, row : row + b + 1, :] = sums[8 * b : 8 * b + b + 1]
    exg[mp, 15:16, :] = jnp.zeros((1, TOK), F32)
    exchange_start(exg, 0)

    lane4 = iota((K, 128), 1) >> 5

    def weigh(w, slab):
        v = g[w, pl.ds(slab * NP, NP)]
        halves = []
        for h in range(2):
            a = [v[4 * h + d] for d in range(4)]
            odd = (lane4 & 1) == 1
            upper = lane4 >= 2
            st = []
            for c in (0, 2):
                st.append(jnp.where(odd, pltpu.roll(a[c + 1], 32, 1), a[c]))
                st.append(jnp.where(odd, a[c + 1], pltpu.roll(a[c], 96, 1)))
            out = [None] * 4
            for c in (0, 1):
                out[c] = jnp.where(upper, pltpu.roll(st[c + 2], 64, 1), st[c])
                out[c + 2] = jnp.where(upper, st[c + 2], pltpu.roll(st[c], 64, 1))
            halves.append(out)
        u = jnp.concatenate(
            [jnp.concatenate([halves[0][i], halves[1][i]], axis=1) for i in range(4)], axis=0
        )
        uu = pieces(split2(u))
        s3 = sb.reshape(16, TOK * STREAMS, 128)
        x = jnp.concatenate([s3[2 * slab], s3[2 * slab + 1]], axis=1)
        d = dot(uu, x, NT)
        pacc[w] += d[:96] + d[96:]
        xb = bb[:, pl.ds(pl.multiple_of(slab * 256, 256), 256)]
        d = dot(uu, xb, NT)
        pbacc[w] += d[:96] + d[96:]

    def own(w, carry):
        weigh(w, z)
        return carry

    lax.fori_loop(0, 2, own, 0)

    def step(m, carry):
        k = 1 + m // 2
        w = m % 2
        before = lax.rem(z + NZ - k, NZ)
        after = lax.rem(z + k, NZ)
        hop(w, k, True, before).wait_recv()

        @pl.when(k < 3)
        def _():
            hop(w, k + 1, True, before).start()

        @pl.when(k == 3)
        def _():
            half_hop(w, True, before).start()

        hop(w, k, False, after).wait_recv()

        @pl.when(k < 3)
        def _():
            hop(w, k + 1, False, after).start()

        @pl.when(k == 3)
        def _():
            half_hop(w, False, after).start()

        def side(n, c):
            weigh(w, lax.rem(z + NZ - k + n * 2 * k, NZ))
            return c

        lax.fori_loop(0, 2, side, 0)
        return carry

    lax.fori_loop(0, 6, step, 0)

    far = lax.rem(z + NZ // 2, NZ)

    def last(w):
        half_hop(w, True, far).wait_recv()
        half_hop(w, False, far).wait_recv()
        weigh(w, far)

    def by_token(v):
        s = dot(pieces(split3(v)), rep4[...], NT)
        return s[0:K] + s[K : 2 * K] + s[2 * K : 3 * K]

    last(0)
    ll = iota((K, TOK * STREAMS), 1) & 3
    sel = pacc[0, 72:96]
    for i in range(3):
        sel = jnp.where(ll == i, pacc[0, 24 * i : 24 * i + 24], sel)
    ex[0, mp] = by_token(sel)
    exchange_start(ex.at[0], 1)
    last(1)

    exchange_wait(exg, 0)
    gt[...] = (exg[0] + exg[1]) + (exg[2] + exg[3])
    exchange_wait(ex.at[0], 1)
    tot0[...] = (ex[0, 0] + ex[0, 1]) + (ex[0, 2] + ex[0, 3])

    sq0 = gram_row(gt, 0, 0) + gram_row(gt, 1, 1) + gram_row(gt, 2, 2) + gram_row(gt, 3, 3)
    inv0 = 1.0 / jnp.sqrt(sq0 / (STREAMS * D) + EPS)

    def logit(k):
        return tot0[k : k + 1, :] * inv0

    post = [2.0 * jax.nn.sigmoid(scale[0] * logit(j) + bias[j]) for j in range(4)]
    res = balance(
        [
            [jnp.exp(scale[1] * logit(4 + 4 * j + i) + bias[4 + 4 * j + i]) for i in range(4)]
            for j in range(4)
        ]
    )
    co = [[res[j][0], res[j][1], res[j][2], res[j][3], post[j]] for j in range(4)]
    for a in range(5):
        for j in range(4):
            cf[8 * a + j : 8 * a + j + 1, :] = co[j][a]
            cf[8 * a + 4 + j : 8 * a + 5 + j, :] = co[j][a]
    hi, lo = spread(cf[...], rep5)
    aexp[0] = hi
    aexp[1] = lo

    both = hi + lo
    rexp = jnp.concatenate([both[:, 256 * b : 256 * b + 128] for b in range(NB)], axis=1)
    acc = rexp[0:1] * pacc[1, 0:24]
    for j in range(1, 4):
        acc = acc + rexp[j : j + 1] * pacc[1, 24 * j : 24 * j + 24]
    raw1 = by_token(acc)
    for j in range(4):
        raw1 = raw1 + post[j] * pbacc[1, 24 * j : 24 * j + 24]
    ex[1, mp] = raw1
    exchange_start(ex.at[1], 2)

    tl = token_of(iota((SR, XR), 1))
    tr = iota((SR, XR), 0) >> 2

    def mix_block(b, carry):
        s3, rows, brows = block_rows(sb, bb, b)
        o3 = ob.reshape(16, TOK * STREAMS, 128)
        at = pl.multiple_of(b * 256, 256)
        parts = []
        for n in range(2):
            v = aexp[n, :, pl.ds(at, 256)]
            full = jnp.concatenate([v] * (SR // 8), axis=0)[:, :XR]
            parts.append(jnp.where(tl == tr, full, 0.0))
        amat = pieces(parts)
        for f in range(8):
            x = jnp.concatenate(
                [
                    jnp.concatenate([s3[2 * f, rows, :], s3[2 * f + 1, rows, :]], axis=1),
                    bb[brows, 256 * f : 256 * f + 256],
                ],
                axis=0,
            )
            d = dot(amat, x, NN)
            d = (d[:SR] + d[SR:]).astype(BF16)
            o3[2 * f, rows, :] = d[:, :128]
            o3[2 * f + 1, rows, :] = d[:, 128:]
        return carry

    lax.fori_loop(0, NB, mix_block, 0)

    exchange_wait(ex.at[1], 2)
    tot1[...] = (ex[1, 0] + ex[1, 1]) + (ex[1, 2] + ex[1, 3])

    for w in range(2):
        for o in range(1, NP):
            plane(w, o, lax.rem(p + o, NP), dp).wait_send()
        for right in (True, False):
            for k in range(1, 4):
                hop(w, k, right, z).wait_send()
            half_hop(w, right, z).wait_send()
    for e, ref in ((0, exg), (1, ex.at[0]), (2, ex.at[1])):
        for o in range(1, NMP):
            exchange(ref, e, o, lax.rem(mp + o, NMP), mp).wait_send()


def finish_kernel(
    sb, bb, ob, tot1, gt, cf, rep5, gain, bias, scale,
    streams_out, branch_in, mix, qexp, nm, obuf, osem, bsem,
):
    outs = [
        pltpu.make_async_copy(ob.at[q], streams_out.at[:, :, pl.ds(q * 128, 128)], osem.at[q])
        for q in range(16)
    ]
    for c in outs:
        c.start()

    a = [[cf[8 * n + j : 8 * n + j + 1, :] for n in range(5)] for j in range(4)]
    sq1 = jnp.zeros((1, TOK), F32)
    for m in range(5):
        for n in range(m, 5):
            s = (a[0][m] * a[0][n] + a[1][m] * a[1][n]) + (a[2][m] * a[2][n] + a[3][m] * a[3][n])
            sq1 = sq1 + (1.0 if m == n else 2.0) * s * gram_row(gt, m, n)
    inv1 = 1.0 / jnp.sqrt(jnp.maximum(sq1, 0.0) / (STREAMS * D) + EPS)

    def logit(k):
        return tot1[k : k + 1, :] * inv1

    pre = [jax.nn.sigmoid(scale[2] * logit(j) + bias[20 + j]) for j in range(4)]
    q = [
        (pre[0] * a[0][n] + pre[1] * a[1][n]) + (pre[2] * a[2][n] + pre[3] * a[3][n])
        for n in range(5)
    ]
    usq = jnp.zeros((1, TOK), F32)
    for m in range(5):
        for n in range(m, 5):
            usq = usq + (1.0 if m == n else 2.0) * (q[m] * q[n]) * gram_row(gt, m, n)
    norm = 1.0 / jnp.sqrt(jnp.maximum(usq, 0.0) / D + EPS)
    q8 = jnp.concatenate([jnp.broadcast_to(v * norm, (8, TOK)) for v in q], axis=0)
    hi, lo = spread(q8, rep5)
    qexp[0] = hi
    qexp[1] = lo

    tl = token_of(iota((TB, XR), 1))
    tr = iota((TB, XR), 0)

    def out_copy(b):
        rows = pl.ds(pl.multiple_of(b * TB, TB), TB)
        return pltpu.make_async_copy(obuf.at[rows], branch_in.at[rows], bsem.at[b])

    def unite_block(b, carry):
        s3, rows, brows = block_rows(sb, bb, b)
        at = pl.multiple_of(b * 256, 256)
        parts = []
        for n in range(2):
            v = qexp[n, :, pl.ds(at, 256)]
            full = jnp.concatenate([v] * (TB // 8), axis=0)[:, :XR]
            parts.append(jnp.where(tl == tr, full, 0.0))
        qmat = pieces(parts)
        for f in range(8):
            x = jnp.concatenate(
                [
                    jnp.concatenate([s3[2 * f, rows, :], s3[2 * f + 1, rows, :]], axis=1),
                    bb[brows, 256 * f : 256 * f + 256],
                ],
                axis=0,
            )
            d = dot(qmat, x, NN)
            d = (d[:TB] + d[TB:]) * gain[0:1, 256 * f : 256 * f + 256]
            obuf[brows, 256 * f : 256 * f + 256] = d.astype(BF16)
        out_copy(b).start()
        return carry

    lax.fori_loop(0, NB, unite_block, 0)

    post = [2.0 * jax.nn.sigmoid(scale[3] * logit(4 + j) + bias[24 + j]) for j in range(4)]
    res = balance(
        [
            [jnp.exp(scale[4] * logit(8 + 4 * j + i) + bias[28 + 4 * j + i]) for i in range(4)]
            for j in range(4)
        ]
    )
    for j in range(4):
        nm[j : j + 1, :] = post[j]
        for i in range(4):
            nm[4 + 4 * j + i : 5 + 4 * j + i, :] = res[j][i]
    nm[20:128, :] = jnp.zeros((108, TOK), F32)
    mix[...] = jnp.transpose(nm[...])[:, :20]

    def drain(b, carry):
        out_copy(b).wait()
        return carry

    lax.fori_loop(0, NB, drain, 0)
    for c in outs:
        c.wait()


def local(streams, branch_out, merge_weight, next_weight, blend_bias, blend_scale, norm_gain):
    vmem = pl.BlockSpec(memory_space=pltpu.VMEM)
    smem = pl.BlockSpec(memory_space=pltpu.SMEM)
    hbm = pl.BlockSpec(memory_space=pltpu.HBM)
    kept = (
        pltpu.VMEM((16, TOK, STREAMS, 128), BF16),
        pltpu.VMEM((TOK, FEAT), BF16),
        pltpu.VMEM((16, TOK, STREAMS, 128), BF16),
        pltpu.VMEM((K, TOK), F32),
        pltpu.VMEM((16, TOK), F32),
        pltpu.VMEM((40, TOK), F32),
        pltpu.VMEM((TOK, NB * 256), BF16),
    )
    dma = pltpu.SemaphoreType.DMA
    state = pl.pallas_call(
        gather_kernel,
        out_shape=kept,
        in_specs=[hbm, hbm, hbm, hbm, smem, smem],
        out_specs=(vmem,) * 7,
        scratch_shapes=[
            pltpu.VMEM((2, NDP, K, 128), F32),
            pltpu.VMEM((2, 4 * K, TOK * STREAMS), F32),
            pltpu.VMEM((2, 4 * K, TOK), F32),
            pltpu.VMEM((TOK, TOK * STREAMS), BF16),
            pltpu.VMEM((20, STREAMS, 32), F32),
            pltpu.VMEM((24, STREAMS, 32), F32),
            pltpu.VMEM((8, NB * 256), F32),
            pltpu.VMEM((2, 8, NB * 256), F32),
            pltpu.VMEM((2, NMP, K, TOK), F32),
            pltpu.VMEM((NMP, 16, TOK), F32),
            pltpu.VMEM((K, TOK), F32),
            dma((19,)),
            dma((2, NP - 1)),
            dma((2, NP - 1)),
            dma((2, 2, 4)),
            dma((2, 2, 4)),
            dma((3, NMP - 1)),
            dma((3, NMP - 1)),
        ],
        compiler_params=pltpu.CompilerParams(
            collective_id=0, has_side_effects=True, vmem_limit_bytes=24 << 20
        ),
        name="gather_mix",
    )(streams, branch_out, merge_weight, next_weight, blend_bias, blend_scale)
    return pl.pallas_call(
        finish_kernel,
        out_shape=(
            jax.ShapeDtypeStruct((TOK, STREAMS, FEAT), BF16),
            jax.ShapeDtypeStruct((TOK, FEAT), BF16),
            jax.ShapeDtypeStruct((TOK, 20), F32),
        ),
        in_specs=[vmem] * 8 + [smem, smem],
        out_specs=(hbm, hbm, vmem),
        scratch_shapes=[
            pltpu.VMEM((2, 8, NB * 256), F32),
            pltpu.VMEM((128, TOK), F32),
            pltpu.VMEM((TOK, FEAT), BF16),
            dma((16,)),
            dma((NB,)),
        ],
        compiler_params=pltpu.CompilerParams(vmem_limit_bytes=16 << 20),
        name="finish",
    )(*state, norm_gain.reshape(1, FEAT), blend_bias, blend_scale)


def solution(mesh):
    placed = (
        P("dp", None, "mp"),
        P("dp", "mp"),
        P(None, None, ("mp", "dp")),
        P(None, None, ("mp", "dp")),
        P(),
        P(),
        P("mp"),
    )
    return jax.shard_map(
        local,
        mesh=mesh,
        in_specs=placed,
        out_specs=(P("dp", None, "mp"), P("dp", "mp"), P("dp", None)),
        check_vma=False,
    )
```

time: 210 us -> 53.8 us (0.26)
  waiting for transfers between devices: 110 us -> 0 us
  Pallas kernels: 0 us -> 45.9 us
  other arithmetic: 24.6 us -> 0 us
  matrix products: 22.1 us -> 0 us
  local copies, waits for them, and re-layouts: 23.5 us -> 6.99 us
  starting transfers between devices: 14.8 us -> 0 us
  between operations: 14.4 us -> 0.67 us
    all_gather x1 -> x0, waiting for transfers between devices: 108 us -> none  [turned_gather(): lax.all_gather(both, axis, axis=0, tiled=True)]
    pallas_call x0 -> x2, Pallas kernels: none -> 45.9 us  [the longest x1 41.9 us: local(): pl.pallas_call(gather_kernel, out_shape=kept, in_specs=[hbm, hbm, hbm, hb...]
    dot_general x3 -> x0, matrix products: 22.1 us -> none  [the longest x1 9.68 us: local(): jnp.einsum('tic,kic->tk', streams, merge_rows, precision=highest, preferr...]
    all_to_all x3 -> x0, starting transfers between devices: 14.8 us -> none  [copy_for_each(): lax.all_to_all(jnp.broadcast_to(x[None], (peers, *x.shape)), axis, 0, 0,...]
    unnamed x24 -> x14, local copies, waits for them, and re-layouts: 13 us -> 6.29 us
    add x2 -> x0, other arithmetic: 6.25 us -> none  [mix_streams(): total + residual_blend[:, target, source, None] * streams[:, source, :].a...]
    convert_element_type x2 -> x0, other arithmetic: 6.13 us -> none  [the longest x1 3.24 us: local(): streams_out = mixed.astype(jnp.bfloat16)]
    reduce_sum x9 -> x0, other arithmetic: 6.1 us -> none  [the longest x1 4.89 us: local(): united_sq = of_everyone(jnp.sum(united * united, axis=1), 'mp')]
  transfers between devices with their start and end apart: 4 -> 0, of which waited for: 2 -> 0; matrix products, arithmetic and copies ran while one was open for 13% -> 0% of each run, Pallas kernels for 0% -> 0%
where the time goes in v1:
time: 53.8 us; the launch traced here: 53.5 us
  Pallas kernels  45.9 us (85%)
  local copies, waits for them, and re-layouts  6.99 us (13%)
  between operations  0.67 us (1%)
    pallas_call x1, Pallas kernels, local(): pl.pallas_call(gather_kernel, out_shape=kept, in_specs=[hbm, hbm, hbm, hb...  41.9 us
    unnamed x14, local copies, waits for them, and re-layouts  6.29 us
    pallas_call x1, Pallas kernels, local(): pl.pallas_call(finish_kernel, out_shape=(jax.ShapeDtypeStruct((TOK, STREA...  4 us

profile of v1, /device:TPU:1, one launch (start us, length us, event | category | flops | bytes accessed | tf_op | source)
XLA Modules:
  0.0 53.5 jit_solution(6183584656185839424)
XLA Ops:
  0.6 0.0 copy-start
  0.6 2.2 %copy-done = bf16[256,4,2048]{2,1,0:T(4,128)(2,1)S(1)} copy-done((bf16[256,4,2048]{2,1,0:T(4,128)(2,1)S(1)}, bf16[256,4,2048]{2,1,0:T(4,128)(2,1)}, u32[]{:S(2)}) %copy-start) | copy-done | bytes 4194328
  2.8 0.0 copy-start.1
  2.8 1.2 %copy-done.1 = bf16[256,2048]{1,0:T(8,128)(2,1)S(1)} copy-done((bf16[256,2048]{1,0:T(8,128)(2,1)S(1)}, bf16[256,2048]{1,0:T(8,128)(2,1)}, u32[]{:S(2)}) %copy-start.1) | copy-done | bytes 1048600
  4.0 0.0 copy-start.2
  4.0 0.8 %copy-done.2 = f32[24,4,32]{2,1,0:T(4,128)S(1)} copy-done((f32[24,4,32]{2,1,0:T(4,128)S(1)}, f32[24,4,32]{2,1,0:T(4,128)}, u32[]{:S(2)}) %copy-start.2) | copy-done | bytes 12312
  4.8 0.0 copy-start.3
  4.8 0.8 %copy-done.3 = f32[20,4,32]{2,1,0:T(4,128)S(1)} copy-done((f32[20,4,32]{2,1,0:T(4,128)S(1)}, f32[20,4,32]{2,1,0:T(4,128)}, u32[]{:S(2)}) %copy-start.3) | copy-done | bytes 10264
  5.6 0.0 copy-start.5
  5.6 0.7 %copy-done.5 = f32[44]{0:T(128)S(1)} copy-done((f32[44]{0:T(128)S(1)}, f32[44]{0:T(128)}, u32[]{:S(2)}) %copy-start.5) | copy-done | bytes 200
  6.3 0.0 copy-start.6
  6.3 0.7 %copy-done.6 = f32[5]{0:T(128)S(1)} copy-done((f32[5]{0:T(128)S(1)}, f32[5]{0:T(128)}, u32[]{:S(2)}) %copy-start.6) | copy-done | bytes 44
  6.9 0.0 copy-start.4
  6.9 41.9 %gather_mix.1 = (bf16[16,256,4,128]{3,2,1,0:T(4,128)(2,1)S(1)}, bf16[256,2048]{1,0:T(8,128)(2,1)S(1)}, bf16[16,256,4,128]{3,2,1,0:T(4,128)(2,1)S(1)}, f32[24,256...) custom-call(bf16[256,4,2048]{2,1,0:T(4,128)(2,1)S(1)} %copy-done, ...), custom_call_target="tpu_custom_call" | custom-call | tf_op jit(solution)/shard_map/gather_mix/pallas_call | solution.py:533
  48.8 0.0 copy-done.4
  48.8 4.0 %finish.1 = (bf16[256,4,2048]{2,1,0:T(4,128)(2,1)}, bf16[256,2048]{1,0:T(8,128)(2,1)}, f32[256,20]{1,0:T(8,128)S(1)}) custom-call(bf16[16,256,4,128]{3,2,1,0:T(4,128)(2,1)S(1)} %get-tuple-element.10.sb, bf16[256,2048]{1,0:T(8,128)(2,1)S(1)} %get-tuple-element.11.bb, bf16[16,256,4,128]{3,2,1,0:T(4,128)(2,1)S(1)} %get-tuple-element.12.ob, ...), custom_call_target="tpu_custom_call" | custom-call | tf_op jit(solution)/shard_map/finish/pallas_call | solution.py:563
  52.8 0.7 %copy.10 = f32[256,20]{0,1:T(8,128)} copy(f32[256,20]{1,0:T(8,128)S(1)} %get-tuple-element.19) | data formatting | bytes 40960 | tf_op jit(solution)/shard_map/finish/pallas_call | solution.py:563
Async XLA Ops:
  0.6 2.2 %copy-start = (bf16[256,4,2048]{2,1,0:T(4,128)(2,1)S(1)}, bf16[256,4,2048]{2,1,0:T(4,128)(2,1)}, u32[]{:S(2)}) copy-start(bf16[256,4,2048]{2,1,0:T(4,128)(2,1)} %s_hbm.1) | copy-start | bytes 12582916
  2.8 1.2 %copy-start.1 = (bf16[256,2048]{1,0:T(8,128)(2,1)S(1)}, bf16[256,2048]{1,0:T(8,128)(2,1)}, u32[]{:S(2)}) copy-start(bf16[256,2048]{1,0:T(8,128)(2,1)} %b_hbm.1) | copy-start | bytes 3145732
  4.0 0.8 %copy-start.2 = (f32[24,4,32]{2,1,0:T(4,128)S(1)}, f32[24,4,32]{2,1,0:T(4,128)}, u32[]{:S(2)}) copy-start(f32[24,4,32]{2,1,0:T(4,128)} %w1_hbm.1) | copy-start | bytes 36868
  4.8 0.8 %copy-start.3 = (f32[20,4,32]{2,1,0:T(4,128)S(1)}, f32[20,4,32]{2,1,0:T(4,128)}, u32[]{:S(2)}) copy-start(f32[20,4,32]{2,1,0:T(4,128)} %w0_hbm.1) | copy-start | bytes 30724
  5.6 0.7 %copy-start.5 = (f32[44]{0:T(128)S(1)}, f32[44]{0:T(128)}, u32[]{:S(2)}) copy-start(f32[44]{0:T(128)} %bias.3) | copy-start | bytes 532
  6.3 0.7 %copy-start.6 = (f32[5]{0:T(128)S(1)}, f32[5]{0:T(128)}, u32[]{:S(2)}) copy-start(f32[5]{0:T(128)} %scale.3) | copy-start | bytes 64
  6.9 41.9 %copy-start.4 = (f32[2048]{0:T(1024)S(1)}, f32[2048]{0:T(1024)}, u32[]{:S(2)}) copy-start(f32[2048]{0:T(1024)} %param.13) | copy-start | bytes 24580

commit v2 on v1

--- a/solution.py
+++ b/solution.py
@@ -103,9 +103,9 @@
 
 
 def gather_kernel(
-    s_hbm, b_hbm, w0_hbm, w1_hbm, bias, scale,
+    s_hbm, b_hbm, w0_hbm, w1_hbm, bias_hbm, scale_hbm,
     sb, bb, ob, tot1, gt, cf, rep5,
-    g, pacc, pbacc, rep4, w0v, w1v, gr, aexp, ex, exg, tot0,
+    g, pacc, pbacc, rep4, w0v, w1v, gr, aexp, ex, exg, tot0, bias, scale,
     in_sem, ps, pr, rs, rr, es, er,
 ):
     dp = lax.axis_index("dp")
@@ -121,6 +121,10 @@
     wcopies = [
         pltpu.make_async_copy(w0_hbm, w0v, in_sem.at[0]),
         pltpu.make_async_copy(w1_hbm, w1v, in_sem.at[1]),
+    ]
+    scopies = [
+        pltpu.make_async_copy(bias_hbm, bias, in_sem.at[19]),
+        pltpu.make_async_copy(scale_hbm, scale, in_sem.at[20]),
     ]
     for c in wcopies:
         c.start()
@@ -143,7 +147,7 @@
         pl.semaphore_signal(
             barrier, inc=1, device_id=dev(dp, lax.rem(mp + o, NMP)), device_id_type=MESH
         )
-    for c in icopies:
+    for c in icopies + scopies:
         c.start()
 
     for c in wcopies:
@@ -214,7 +218,7 @@
     pacc[...] = jnp.zeros_like(pacc)
     pbacc[...] = jnp.zeros_like(pbacc)
     gr[...] = jnp.zeros_like(gr)
-    for c in icopies:
+    for c in icopies + scopies:
         c.wait()
 
     plane_wait(0)
@@ -426,7 +430,7 @@
 
 def finish_kernel(
     sb, bb, ob, tot1, gt, cf, rep5, gain, bias, scale,
-    streams_out, branch_in, mix, qexp, nm, obuf, osem, bsem,
+    streams_out, branch_in, mix, qexp, obuf, osem, bsem,
 ):
     outs = [
         pltpu.make_async_copy(ob.at[q], streams_out.at[:, :, pl.ds(q * 128, 128)], osem.at[q])
@@ -501,11 +505,9 @@
         ]
     )
     for j in range(4):
-        nm[j : j + 1, :] = post[j]
+        mix[j : j + 1, :] = post[j]
         for i in range(4):
-            nm[4 + 4 * j + i : 5 + 4 * j + i, :] = res[j][i]
-    nm[20:128, :] = jnp.zeros((108, TOK), F32)
-    mix[...] = jnp.transpose(nm[...])[:, :20]
+            mix[4 + 4 * j + i : 5 + 4 * j + i, :] = res[j][i]
 
     def drain(b, carry):
         out_copy(b).wait()
@@ -530,10 +532,14 @@
         pltpu.VMEM((TOK, NB * 256), BF16),
     )
     dma = pltpu.SemaphoreType.DMA
+    given = tuple(
+        pltpu.with_memory_space_constraint(v, pltpu.HBM)
+        for v in (streams, branch_out, merge_weight, next_weight, blend_bias, blend_scale)
+    )
     state = pl.pallas_call(
         gather_kernel,
         out_shape=kept,
-        in_specs=[hbm, hbm, hbm, hbm, smem, smem],
+        in_specs=[hbm] * 6,
         out_specs=(vmem,) * 7,
         scratch_shapes=[
             pltpu.VMEM((2, NDP, K, 128), F32),
@@ -547,7 +553,9 @@
             pltpu.VMEM((2, NMP, K, TOK), F32),
             pltpu.VMEM((NMP, 16, TOK), F32),
             pltpu.VMEM((K, TOK), F32),
-            dma((19,)),
+            pltpu.SMEM((44,), F32),
+            pltpu.SMEM((5,), F32),
+            dma((21,)),
             dma((2, NP - 1)),
             dma((2, NP - 1)),
             dma((2, 2, 4)),
@@ -559,19 +567,18 @@
             collective_id=0, has_side_effects=True, vmem_limit_bytes=24 << 20
         ),
         name="gather_mix",
-    )(streams, branch_out, merge_weight, next_weight, blend_bias, blend_scale)
-    return pl.pallas_call(
+    )(*given)
+    streams_out, branch_in, mix = pl.pallas_call(
         finish_kernel,
         out_shape=(
             jax.ShapeDtypeStruct((TOK, STREAMS, FEAT), BF16),
             jax.ShapeDtypeStruct((TOK, FEAT), BF16),
-            jax.ShapeDtypeStruct((TOK, 20), F32),
+            jax.ShapeDtypeStruct((20, TOK), F32),
         ),
         in_specs=[vmem] * 8 + [smem, smem],
         out_specs=(hbm, hbm, vmem),
         scratch_shapes=[
             pltpu.VMEM((2, 8, NB * 256), F32),
-            pltpu.VMEM((128, TOK), F32),
             pltpu.VMEM((TOK, FEAT), BF16),
             dma((16,)),
             dma((NB,)),
@@ -579,6 +586,7 @@
         compiler_params=pltpu.CompilerParams(vmem_limit_bytes=16 << 20),
         name="finish",
     )(*state, norm_gain.reshape(1, FEAT), blend_bias, blend_scale)
+    return streams_out, branch_in, mix.T
 
 
 def solution(mesh):

time: 53.8 us -> 45.9 us (0.85)
  local copies, waits for them, and re-layouts: 6.99 us -> 0.01 us
  Pallas kernels: 45.9 us -> 45.1 us
    unnamed x14 -> x6, local copies, waits for them, and re-layouts: 6.29 us -> 0.01 us
    pallas_call x1, Pallas kernels: 41.9 us -> 40.5 us  [local(): pl.pallas_call(gather_kernel, out_shape=kept, in_specs=[hbm] * 6, out_spe...]
    pallas_call x1 -> x0, local copies, waits for them, and re-layouts: 0.69 us -> none  [local(): pl.pallas_call(finish_kernel, out_shape=(jax.ShapeDtypeStruct((TOK, STREA...]
    pallas_call x1, Pallas kernels: 4 us -> 4.61 us  [local(): pl.pallas_call(finish_kernel, out_shape=(jax.ShapeDtypeStruct((TOK, STREA...]
where the time goes in v2:
time: 45.9 us; the launch traced here: 45.8 us
  Pallas kernels  45.1 us (98%)
  between operations  0.69 us (2%)
    pallas_call x1, Pallas kernels, local(): pl.pallas_call(gather_kernel, out_shape=kept, in_specs=[hbm] * 6, out_spe...  40.5 us
    pallas_call x1, Pallas kernels, local(): pl.pallas_call(finish_kernel, out_shape=(jax.ShapeDtypeStruct((TOK, STREA...  4.61 us

profile of v2, /device:TPU:1, one launch (start us, length us, event | category | flops | bytes accessed | tf_op | source)
XLA Modules:
  0.0 45.8 jit_solution(2513982297942851824)
XLA Ops:
  0.6 0.0 copy-start.2
  0.6 0.0 copy-start.1
  0.7 0.0 copy-start
  0.7 40.5 %gather_mix.1 = (bf16[16,256,4,128]{3,2,1,0:T(4,128)(2,1)S(1)}, bf16[256,2048]{1,0:T(8,128)(2,1)S(1)}, bf16[16,256,4,128]{3,2,1,0:T(4,128)(2,1)S(1)}, f32[24,256...) custom-call(bf16[256,4,2048]{2,1,0:T(4,128)(2,1)} %s_hbm.1, ...), custom_call_target="tpu_custom_call" | custom-call | tf_op jit(solution)/shard_map/gather_mix/pallas_call | solution.py:539
  41.2 0.0 copy-done.2
  41.2 0.0 copy-done.1
  41.2 0.0 copy-done
  41.2 4.6 %finish.1 = (bf16[256,4,2048]{2,1,0:T(4,128)(2,1)}, bf16[256,2048]{1,0:T(8,128)(2,1)}, f32[20,256]{1,0:T(8,128)}) custom-call(bf16[16,256,4,128]{3,2,1,0:T(4,128)(2,1)S(1)} %get-tuple-element.13.sb, bf16[256,2048]{1,0:T(8,128)(2,1)S(1)} %get-tuple-element.14.bb, bf16[16,256,4,128]{3,2,1,0:T(4,128)(2,1)S(1)} %get-tuple-element.15.ob, ...), custom_call_target="tpu_custom_call" | custom-call | tf_op jit(solution)/shard_map/finish/pallas_call | solution.py:571
Async XLA Ops:
  0.6 40.5 %copy-start.2 = (f32[5]{0:T(128)S(1)}, f32[5]{0:T(128)}, u32[]{:S(2)}) copy-start(f32[5]{0:T(128)} %scale.1) | copy-start | bytes 64
  0.6 40.5 %copy-start.1 = (f32[44]{0:T(128)S(1)}, f32[44]{0:T(128)}, u32[]{:S(2)}) copy-start(f32[44]{0:T(128)} %bias.1) | copy-start | bytes 532
  0.7 40.5 %copy-start = (f32[2048]{0:T(1024)S(1)}, f32[2048]{0:T(1024)}, u32[]{:S(2)}) copy-start(f32[2048]{0:T(1024)} %param.13) | copy-start | bytes 24580
